TPU v7x, 256 devices: a whole 4x4x8 slice. The times are simulated.
256 devices in a mesh: band: 4 (over x), dom: 64 (over y, z, core).
Axes of the slice: x: 4, y: 4, z: 8, core: 2. Of those that a mesh axis runs over, the one named last changes fastest.
Arguments:
- orbitals: float32 [128, 32, 32, 1024], P('dom', None, None, 'band'), may hold values from -6 to 6
- potential: float32 [128, 32, 32], P('dom'), may hold values from -2 to 2
- projectors: float32 [8192, 8, 256], P('dom'), may hold values from -0.375 to 0.375
- tile_cells: int32 [8192, 256], P('dom'), may hold values from 0 to 2047
- tile_atom: int32 [8192], replicated, may hold values from -1 to 511, as said below
- atom_owner: int32 [512], replicated, may hold values from 0 to 511, as said below
- coupling: float32 [512, 8, 8], P('dom'), may hold values from -2 to 2
- rotation: float32 [1024, 1024], P(None, 'band'), may hold values from -0.1875 to 0.1875
Outputs:
- rotated_orbitals: float32 [128, 32, 32, 1024], P('dom', None, None, 'band')
- rotated_applied: float32 [128, 32, 32, 1024], P('dom', None, None, 'band')
Inputs may be any that keep to these rules, and one draw needn't show every extreme that they name: `tile_atom`: tile slots come in blocks of 128, one block a domain; in each block the used slots come first, at least half of them are used, and some block is full. An atom a is owned by domain atom_owner[a] // 8. The tiles of one domain name atoms of any one owning domain at most 4 times, and some owning domain is named exactly 4 times by every domain. `atom_owner`: each row of the coupling table belongs to exactly one atom.
All inputs are finite; a program needn't handle non-finite values.
Results may differ from a plain program's by a relative error of at most 0.000071.
Values sent between devices are 32-bit elements; how exact they have to be, the bound alone decides.
No kernel may reach another device: no remote copies, remote signals or barrier semaphores. Data moves between devices by JAX's collectives and lax.ppermute only.
A program may use at most 128 MiB of HBM per device.

v0:
```python
import jax
import jax.numpy as jnp
from jax import lax
from jax.sharding import PartitionSpec as P


def padded_2(cells, sides, width):
    for axis, dim in sides:
        count = lax.axis_size(axis)
        head = lax.slice_in_dim(cells, 0, width, axis=dim)
        tail = lax.slice_in_dim(cells, cells.shape[dim] - width, cells.shape[dim], axis=dim)
        cells = jnp.concatenate(
            [
                lax.ppermute(tail, axis, [(i, (i + 1) % count) for i in range(count)]),
                cells,
                lax.ppermute(head, axis, [((i + 1) % count, i) for i in range(count)]),
            ],
            axis=dim,
        )
    return cells


def owner_rows(atom_ids, atom_owner):
    match = atom_ids[..., None] == jnp.arange(atom_owner.shape[0], dtype=jnp.int32)
    found_rows = jnp.sum(jnp.where(match, atom_owner, 0), axis=-1)
    return jnp.where(atom_ids >= 0, found_rows, -1)


def body(orbitals, potential, projectors, tile_cells, tile_atom, atom_owner, coupling, rotation):
    plane_count, rows_y, rows_z, band_count = orbitals.shape
    cell_count = plane_count * rows_y * rows_z
    entry_count, proj_count, tile_size = projectors.shape
    atom_total = atom_owner.shape[0]
    domain_index = lax.axis_index("dom")
    padded = padded_2(orbitals, (("dom", 0),), 1)
    beside = padded[2:] + padded[:-2]
    beside = beside + jnp.roll(orbitals, 1, 1) + jnp.roll(orbitals, -1, 1)
    beside = beside + jnp.roll(orbitals, 1, 2) + jnp.roll(orbitals, -1, 2)
    applied_local = (3.0 + potential[..., None]) * orbitals - 0.5 * beside
    flat_field = orbitals.reshape(cell_count, band_count)
    block_size = min(16, entry_count)
    block_count = entry_count // block_size
    cell_blocks = tile_cells.reshape(block_count, block_size, tile_size)
    value_blocks = projectors.reshape(block_count, block_size, proj_count, tile_size)
    cell_ids = jnp.arange(cell_count, dtype=jnp.int32)

    def densify(inputs):
        tile_index, values = inputs
        one_hot = (tile_index[..., None] == cell_ids).astype(jnp.float32)
        return jnp.einsum("ekt,etc->ekc", values, one_hot, precision=lax.Precision.HIGHEST)

    dense_proj = lax.map(densify, (cell_blocks, value_blocks)).reshape(
        entry_count * proj_count, cell_count
    )
    partials = jnp.dot(
        dense_proj, flat_field, precision=lax.Precision.HIGHEST, preferred_element_type=jnp.float32
    )
    partials = partials.reshape(entry_count, proj_count, band_count)
    my_atoms = lax.dynamic_slice_in_dim(tile_atom, domain_index * entry_count, entry_count)
    my_rows = owner_rows(my_atoms, atom_owner)
    row_match = (my_rows[:, None] == jnp.arange(atom_total, dtype=jnp.int32)[None, :]).astype(
        jnp.float32
    )
    columns = row_match
    owned_sums = lax.psum_scatter(
        jnp.einsum("ea,ekb->akb", columns, partials, precision=lax.Precision.HIGHEST),
        "dom",
        scatter_dimension=0,
        tiled=True,
    )
    scaled = jnp.einsum("akj,ajb->akb", coupling, owned_sums, precision=lax.Precision.HIGHEST)
    columns = row_match
    returned = jnp.einsum(
        "ea,akb->ekb",
        columns,
        lax.all_gather(scaled, "dom", axis=0, tiled=True),
        precision=lax.Precision.HIGHEST,
    )
    returned_rows = returned.reshape(entry_count * proj_count, band_count)
    applied_far = jnp.einsum(
        "rc,rb->cb", dense_proj, returned_rows, precision=lax.Precision.HIGHEST
    )
    applied = applied_local + applied_far.reshape(orbitals.shape)
    full_rotation = lax.all_gather(rotation, "band", axis=1, tiled=True)
    first_turned = jnp.einsum(
        "xyzb,bc->xyzc",
        lax.all_to_all(orbitals, "band", split_axis=1, concat_axis=3, tiled=True),
        full_rotation,
        precision=lax.Precision.HIGHEST,
    )
    second_turned = jnp.einsum(
        "xyzb,bc->xyzc",
        lax.all_to_all(applied, "band", split_axis=1, concat_axis=3, tiled=True),
        full_rotation,
        precision=lax.Precision.HIGHEST,
    )
    rotated_orbitals = lax.all_to_all(first_turned, "band", split_axis=3, concat_axis=1, tiled=True)
    rotated_applied = lax.all_to_all(second_turned, "band", split_axis=3, concat_axis=1, tiled=True)
    return (rotated_orbitals, rotated_applied)


def solution(mesh):
    return jax.shard_map(
        body,
        mesh=mesh,
        in_specs=(
            P("dom", None, None, "band"),
            P("dom", None, None),
            P("dom", None, None),
            P("dom", None),
            P(),
            P(),
            P("dom", None, None),
            P(None, "band"),
        ),
        out_specs=(P("dom", None, None, "band"), P("dom", None, None, "band")),
        check_vma=False,
    )
```

profile of v0, /device:TPU:40, one launch (start us, length us, event | category | flops | bytes accessed | tf_op | source)
XLA Modules:
  0.0 543.7 jit_solution(14078225057063549570)
XLA Ops:
  7.2 0.8 dynamic_slice.11
  8.0 0.9 select_reduce_fusion
  8.9 0.8 compare_select_fusion
  9.6 104.5 %while.11 = (s32[]{:T(128)}, f32[8,16,8,2048]{3,2,1,0:T(8,128)}, f32[8,16,8,256]{3,2,1,0:T(8,128)}, s32[8,16,256]{2,1,0:T(8,128)}, s32[]{:T(128)}) while((s32[]{:T(128)}, f32[8,16,8,2048]{3,2,1,0:T(8,128)}, f32[8,16,8,256]{3,2,1,0:T(8,128)}, s32[8,16,256]{2,1,0:T(8,128)}, s32[]{:T(128)}) %tuple.40), condition=%wide.region_1.2_spmd.clone, body=%wide.region_0.1_spmd.clone.sunk | while | flops 813694976 | bytes 1229889 | solution.py:52
  9.6 0.9 dynamic-slice_bitcast_fusion.2
  10.5 12.3 %fusion.48 = f32[8,16,8,2048]{3,2,1,0:T(8,128)} fusion(f32[8,16,8,2048]{3,2,1,0:T(8,128)} %get-tuple-element.89, s32[]{:T(128)} %get-tuple-element.88, s32[16,256]{1,0:T(8,128)S(1)} %dynamic-slice_bitcast_fusion.2, f32[8,16,8,256]{3,2,1,0:T(8,128)} %get-tuple-element.95), kind=kOutput, calls=%fused_computation.5.clone.1 | convolution fusion | flops 813694976 | bytes 1197056 | tf_op jit(solution)/shard_map/while/body/eval_jaxpr/ekt,etc->ekc/dot_general | solution.py:50
  23.6 12.3 %fusion.48 = f32[8,16,8,2048]{3,2,1,0:T(8,128)} fusion(f32[8,16,8,2048]{3,2,1,0:T(8,128)} %get-tuple-element.89, s32[]{:T(128)} %get-tuple-element.88, s32[16,256]{1,0:T(8,128)S(1)} %dynamic-slice_bitcast_fusion.2, f32[8,16,8,256]{3,2,1,0:T(8,128)} %get-tuple-element.95), kind=kOutput, calls=%fused_computation.5.clone.1 | convolution fusion | flops 813694976 | bytes 1197056 | tf_op jit(solution)/shard_map/while/body/eval_jaxpr/ekt,etc->ekc/dot_general | solution.py:50
  36.6 12.3 %fusion.48 = f32[8,16,8,2048]{3,2,1,0:T(8,128)} fusion(f32[8,16,8,2048]{3,2,1,0:T(8,128)} %get-tuple-element.89, s32[]{:T(128)} %get-tuple-element.88, s32[16,256]{1,0:T(8,128)S(1)} %dynamic-slice_bitcast_fusion.2, f32[8,16,8,256]{3,2,1,0:T(8,128)} %get-tuple-element.95), kind=kOutput, calls=%fused_computation.5.clone.1 | convolution fusion | flops 813694976 | bytes 1197056 | tf_op jit(solution)/shard_map/while/body/eval_jaxpr/ekt,etc->ekc/dot_general | solution.py:50
  49.6 12.3 %fusion.48 = f32[8,16,8,2048]{3,2,1,0:T(8,128)} fusion(f32[8,16,8,2048]{3,2,1,0:T(8,128)} %get-tuple-element.89, s32[]{:T(128)} %get-tuple-element.88, s32[16,256]{1,0:T(8,128)S(1)} %dynamic-slice_bitcast_fusion.2, f32[8,16,8,256]{3,2,1,0:T(8,128)} %get-tuple-element.95), kind=kOutput, calls=%fused_computation.5.clone.1 | convolution fusion | flops 813694976 | bytes 1197056 | tf_op jit(solution)/shard_map/while/body/eval_jaxpr/ekt,etc->ekc/dot_general | solution.py:50
  62.7 12.3 %fusion.48 = f32[8,16,8,2048]{3,2,1,0:T(8,128)} fusion(f32[8,16,8,2048]{3,2,1,0:T(8,128)} %get-tuple-element.89, s32[]{:T(128)} %get-tuple-element.88, s32[16,256]{1,0:T(8,128)S(1)} %dynamic-slice_bitcast_fusion.2, f32[8,16,8,256]{3,2,1,0:T(8,128)} %get-tuple-element.95), kind=kOutput, calls=%fused_computation.5.clone.1 | convolution fusion | flops 813694976 | bytes 1197056 | tf_op jit(solution)/shard_map/while/body/eval_jaxpr/ekt,etc->ekc/dot_general | solution.py:50
  75.7 12.3 %fusion.48 = f32[8,16,8,2048]{3,2,1,0:T(8,128)} fusion(f32[8,16,8,2048]{3,2,1,0:T(8,128)} %get-tuple-element.89, s32[]{:T(128)} %get-tuple-element.88, s32[16,256]{1,0:T(8,128)S(1)} %dynamic-slice_bitcast_fusion.2, f32[8,16,8,256]{3,2,1,0:T(8,128)} %get-tuple-element.95), kind=kOutput, calls=%fused_computation.5.clone.1 | convolution fusion | flops 813694976 | bytes 1197056 | tf_op jit(solution)/shard_map/while/body/eval_jaxpr/ekt,etc->ekc/dot_general | solution.py:50
  88.8 12.3 %fusion.48 = f32[8,16,8,2048]{3,2,1,0:T(8,128)} fusion(f32[8,16,8,2048]{3,2,1,0:T(8,128)} %get-tuple-element.89, s32[]{:T(128)} %get-tuple-element.88, s32[16,256]{1,0:T(8,128)S(1)} %dynamic-slice_bitcast_fusion.2, f32[8,16,8,256]{3,2,1,0:T(8,128)} %get-tuple-element.95), kind=kOutput, calls=%fused_computation.5.clone.1 | convolution fusion | flops 813694976 | bytes 1197056 | tf_op jit(solution)/shard_map/while/body/eval_jaxpr/ekt,etc->ekc/dot_general | solution.py:50
  101.9 12.3 %fusion.48 = f32[8,16,8,2048]{3,2,1,0:T(8,128)} fusion(f32[8,16,8,2048]{3,2,1,0:T(8,128)} %get-tuple-element.89, s32[]{:T(128)} %get-tuple-element.88, s32[16,256]{1,0:T(8,128)S(1)} %dynamic-slice_bitcast_fusion.2, f32[8,16,8,256]{3,2,1,0:T(8,128)} %get-tuple-element.95), kind=kOutput, calls=%fused_computation.5.clone.1 | convolution fusion | flops 813694976 | bytes 1197056 | tf_op jit(solution)/shard_map/while/body/eval_jaxpr/ekt,etc->ekc/dot_general | solution.py:50
  114.2 9.1 %fusion.38 = f32[128,8,256]{2,1,0:T(8,128)S(1)} fusion(f32[128,8,2048]{2,1,0:T(8,128)} %bitcast.78, f32[2048,256,1]{1,0,2:T(8,128)S(1)} %bitcast.72), kind=kOutput, calls=%fused_computation.47 | convolution fusion | flops 6442450944 | bytes 11534336 | tf_op jit(solution)/shard_map/dot_general | solution.py:55
  123.3 3.9 fusion.25
  127.3 145.6 %reduce-scatter.2.cloned.1.call-done = f32[8,8,256]{2,0,1:T(8,128)} async-done(((f32[512,8,256]{2,0,1:T(8,128)}), f32[8,8,256]{2,0,1:T(8,128)}) %reduce-scatter.2.cloned.1.call-update) | async-done | bytes 65552 | tf_op jit(solution)/shard_map/reduce_scatter | solution.py:65
  272.9 1.6 convolution_bitcast_fusion
  275.3 1.7 fusion.37
  277.6 1.6 copy.49
  279.2 4.5 all-to-all-start
  283.7 9.3 %copy.53 = f32[2048,1024]{1,0:T(8,128)} copy(f32[2048,1024]{0,1:T(8,128)} %bitcast.79) | data formatting | bytes 16777216 | tf_op jit(solution)/shard_map/rc,rb->cb/dot_general | solution.py:80
  293.2 2.5 fusion.33
  295.6 2.5 fusion.35
  298.2 54.4 %all-gather.5.cloned.1.call-done = f32[512,8,256]{2,1,0:T(8,128)} async-done(((f32[8,8,256]{2,1,0:T(8,128)}), f32[512,8,256]{2,1,0:T(8,128)}) %all-gather.5.cloned.1.call-update) | async-done | bytes 4194320 | tf_op jit(solution)/shard_map/all_gather | solution.py:76
  352.6 5.1 fusion.13
  357.7 12.5 %fusion.22 = f32[2,32,32,256]{3,2,1,0:T(8,128)S(1)} fusion(f32[2,32,32,256]{3,2,1,0:T(8,128)S(1)} %copy-done.2, f32[1,32,32,256]{3,2,1,0:T(8,128)} %collective-permute-done.1, f32[1,32,32,256]{3,2,1,0:T(8,128)S(1)} %collective-permute-done, f32[2,31,32,256]{3,2,1,0:T(8,128)} %get-tuple-element.53, f32[2,1,32,256]{3,2,1,0:T(8,128)S(1)} %get-tuple-element.55, ...), kind=kOutput, calls=%fused_computation.24 | convolution fusion | flops 6450315264 | bytes 24125440 | tf_op jit(solution)/shard_map/rc,rb->cb/dot_general | solution.py:80
  370.2 1.5 copy.59
  371.7 4.5 all-to-all-start.2
  376.2 4.3 copy.80
  380.5 3.3 all_to_all.55
  383.8 43.0 %all-gather.3.cloned.1.call-done = f32[1024,1024]{1,0:T(8,128)} async-done(((f32[1024,256]{1,0:T(8,128)}), f32[1024,1024]{1,0:T(8,128)}) %all-gather.3.cloned.1.call-update) | async-done | bytes 4194320 | tf_op jit(solution)/shard_map/all_gather | solution.py:84
  426.8 10.2 %fusion.11 = f32[2,8,32,1024]{3,2,1,0:T(8,128)} fusion(f32[2,8,32,1024]{3,2,1,0:T(8,128)} %all_to_all.55, f32[1024,1024]{1,0:T(8,128)} %all-gather.3.cloned.1.call-done), kind=kOutput, calls=%fused_computation.12 | convolution fusion | flops 6442450944 | bytes 8388608 | tf_op jit(solution)/shard_map/xyzb,bc->xyzc/dot_general | solution.py:85
  437.0 7.5 %copy.51 = f32[2,8,32,1024]{2,1,0,3:T(8,128)} copy(f32[2,8,32,1024]{3,2,1,0:T(8,128)} %fusion.11) | data formatting | bytes 4194304 | tf_op jit(solution)/shard_map/xyzb,bc->xyzc/dot_general | solution.py:85
  444.5 7.1 %reshape.41 = f32[4,1,131072]{2,1,0:T(1,128)} reshape(f32[1024,2,8,32]{3,2,1,0:T(8,128)} %bitcast.73) | data formatting | bytes 4194304
  451.6 4.7 all-to-all-start.1
  456.3 2.7 copy.79
  459.1 3.3 all_to_all.63
  462.4 9.6 %fusion.9 = f32[2,8,32,1024]{3,2,1,0:T(8,128)S(1)} fusion(f32[2,8,32,1024]{3,2,1,0:T(8,128)} %all_to_all.63, f32[1024,1024]{1,0:T(8,128)} %all-gather.3.cloned.1.call-done), kind=kOutput, calls=%fused_computation.10 | convolution fusion | flops 6442450944 | bytes 8388608 | tf_op jit(solution)/shard_map/xyzb,bc->xyzc/dot_general | solution.py:91
  472.0 6.2 %copy.61 = f32[2,8,32,1024]{2,1,0,3:T(8,128)} copy(f32[2,8,32,1024]{3,2,1,0:T(8,128)S(1)} %fusion.9) | data formatting | bytes 4194304 | tf_op jit(solution)/shard_map/xyzb,bc->xyzc/dot_general | solution.py:91
  478.3 7.1 %reshape.43 = f32[4,1,131072]{2,1,0:T(1,128)} reshape(f32[1024,2,8,32]{3,2,1,0:T(8,128)} %bitcast.74) | data formatting | bytes 4194304
  485.4 5.2 all-to-all-start.3
  491.1 7.7 %reduce = f32[4,131072]{1,0:T(4,128)S(1)} reduce(f32[4,1,131072]{2,1,0:T(1,128)} %all-to-all-done.1, f32[]{:T(128)} %broadcast.5), dimensions={1}, to_apply=%all_to_all.56.reduce_sub_computation | reduce | bytes 4194308 | tf_op jit(solution)/shard_map/all_to_all | solution.py:97
  498.9 6.1 %reshape.42 = f32[1024,2,8,32]{3,2,1,0:T(8,128)} reshape(f32[4,131072]{1,0:T(4,128)S(1)} %reduce) | data formatting | bytes 4194304
  505.0 6.4 %copy.52 = f32[2,4,8,32,256]{4,3,2,1,0:T(8,128)} copy(f32[2,4,8,32,256]{3,2,0,4,1:T(8,128)} %bitcast.75) | data formatting | bytes 4194304 | tf_op jit(solution)/shard_map/all_to_all | solution.py:97
  511.4 5.4 all-to-all-done.3
  516.8 7.7 %reduce.1 = f32[4,131072]{1,0:T(4,128)S(1)} reduce(f32[4,1,131072]{2,1,0:T(1,128)} %all-to-all-done.3, f32[]{:T(128)} %broadcast.5), dimensions={1}, to_apply=%all_to_all.64.reduce_sub_computation | reduce | bytes 4194308 | tf_op jit(solution)/shard_map/all_to_all | solution.py:98
  524.5 6.1 %reshape.44 = f32[1024,2,8,32]{3,2,1,0:T(8,128)} reshape(f32[4,131072]{1,0:T(4,128)S(1)} %reduce.1) | data formatting | bytes 4194304
  530.7 6.3 %copy.62 = f32[2,4,8,32,256]{4,3,2,1,0:T(8,128)} copy(f32[2,4,8,32,256]{3,2,0,4,1:T(8,128)} %bitcast.76) | data formatting | bytes 4194304 | tf_op jit(solution)/shard_map/all_to_all | solution.py:98
  (37 shorter events, 7.2 us)
Async XLA Ops:
  7.2 265.7 %copy-start = (f32[8,8,8]{2,1,0:T(8,128)S(1)}, f32[8,8,8]{2,1,0:T(8,128)}, u32[]{:S(2)}) copy-start(f32[8,8,8]{2,1,0:T(8,128)} %param.16) | copy-start | bytes 6148
  7.2 265.7 %reduce-scatter.2.cloned.1.call-start = ((), (), s32[]{:S(2)}) async-start(), calls=%async_computation.6 | async-start | bytes 4259840 | tf_op jit(solution)/shard_map/reduce_scatter | solution.py:65
  9.6 104.6 %copy-start.2 = (f32[2,32,32,256]{3,2,1,0:T(8,128)S(1)}, f32[2,32,32,256]{3,2,1,0:T(8,128)}, u32[]{:S(2)}) copy-start(f32[2,32,32,256]{3,2,1,0:T(8,128)} %param.10) | copy-start | bytes 6291460
  127.2 225.3 %all-gather.5.cloned.1.call-start = ((), (), s32[]{:S(2)}) async-start(), calls=%async_computation.7 | async-start | bytes 4259840 | tf_op jit(solution)/shard_map/all_gather | solution.py:76
  274.5 152.2 %all-gather.3.cloned.1.call-start = ((), (), s32[]{:S(2)}) async-start(), calls=%async_computation.5 | async-start | bytes 5242880 | tf_op jit(solution)/shard_map/all_gather | solution.py:84
  277.0 80.7 %collective-permute-start = (f32[1,32,32,256]{3,2,1,0:T(8,128)}, f32[1,32,32,256]{3,2,1,0:T(8,128)S(1)}, u32[]{:S(2)}, u32[]{:S(2)}) collective-permute-start(f32[1,32,32,256]{3,2,1,0:T(8,128)} %get-tuple-element.56), channel_id=1, source_target_pairs={{1,0},{2,1},{3,2},{4,3},{5,4},{6,5},{7,6},{8,7},{9,8},{10,9},{11,1... | collective-permute-start | bytes 3145736 | tf_op jit(solution)/shard_map/ppermute | solution.py:16
  277.1 80.5 %collective-permute-start.1 = (f32[1,32,32,256]{3,2,1,0:T(8,128)}, f32[1,32,32,256]{3,2,1,0:T(8,128)}, u32[]{:S(2)}, u32[]{:S(2)}) collective-permute-start(f32[1,32,32,256]{3,2,1,0:T(8,128)} %get-tuple-element.57), channel_id=1, source_target_pairs={{0,1},{1,2},{2,3},{3,4},{4,5},{5,6},{6,7},{7,8},{8,9},{9,10},{10,1... | collective-permute-start | bytes 3145736 | tf_op jit(solution)/shard_map/ppermute | solution.py:14
  279.2 92.5 %all-to-all-start = ((f32[2,32,32,256]{3,2,0,1:T(8,128)}), f32[2,32,32,256]{3,2,0,1:T(8,128)}, u32[]{:S(2)}, u32[]{:S(2)}) async-start(f32[2,32,32,256]{3,2,0,1:T(8,128)} %copy.49), calls=%async_computation | async-start | bytes 4194304 | tf_op jit(solution)/shard_map/all_to_all | solution.py:87
  283.7 9.3 %copy-start.5 = (f32[2,32,32]{2,1,0:T(8,128)S(1)}, f32[2,32,32]{2,1,0:T(8,128)}, u32[]{:S(2)}) copy-start(f32[2,32,32]{2,1,0:T(8,128)} %param.11) | copy-start | bytes 24580
  352.6 5.1 copy-start.3
  352.6 5.1 copy-start.4
  371.7 79.9 %all-to-all-start.2 = ((f32[2,32,32,256]{3,2,0,1:T(8,128)}), f32[2,32,32,256]{3,2,0,1:T(8,128)S(1)}, u32[]{:S(2)}, u32[]{:S(2)}) async-start(f32[2,32,32,256]{3,2,0,1:T(8,128)} %copy.59), calls=%async_computation.3 | async-start | bytes 4194304 | tf_op jit(solution)/shard_map/all_to_all | solution.py:93
  451.6 33.8 %all-to-all-start.1 = ((f32[4,1,131072]{2,1,0:T(1,128)}), f32[4,1,131072]{2,1,0:T(1,128)}, u32[]{:S(2)}, u32[]{:S(2)}) async-start(f32[4,1,131072]{2,1,0:T(1,128)} %reshape.41), calls=%async_computation.1 | async-start | bytes 4194304 | tf_op jit(solution)/shard_map/all_to_all | solution.py:97
  485.4 31.5 %all-to-all-start.3 = ((f32[4,1,131072]{2,1,0:T(1,128)}), f32[4,1,131072]{2,1,0:T(1,128)}, u32[]{:S(2)}, u32[]{:S(2)}) async-start(f32[4,1,131072]{2,1,0:T(1,128)} %reshape.43), calls=%async_computation.4 | async-start | bytes 4194304 | tf_op jit(solution)/shard_map/all_to_all | solution.py:98
  530.7 6.3 %copy-start.1 = (f32[8,8,8]{2,1,0:T(8,128)S(1)}, f32[8,8,8]{2,1,0:T(8,128)}, u32[]{:S(2)}) copy-start(f32[8,8,8]{2,1,0:T(8,128)} %param.16) | copy-start | bytes 6148
Sparse Core Ops, SparseCore 0:
  127.4 145.4 reduce-scatter.1
  275.6 76.8 all-gather.4
  354.4 72.3 all-gather.2
where the time goes:
time: 554 us; the launch traced here: 544 us
  waiting for transfers between devices  249 us (45%)
  matrix products  151 us (27%)
  local copies, waits for them, and re-layouts  92.9 us (17%)
  starting transfers between devices  19.7 us (4%)
  other arithmetic  17.1 us (3%)
  between operations  14.1 us (3%)
    reduce_scatter x1, waiting for transfers between devices, body(): lax.psum_scatter(jnp.einsum('ea,ekb->akb', columns, partials, precision=l...  146 us
    dot_general x8, matrix products, densify(): jnp.einsum('ekt,etc->ekc', values, one_hot, precision=lax.Precision.HIGHEST)  98.6 us
    all_gather x1, waiting for transfers between devices, body(): lax.all_gather(scaled, 'dom', axis=0, tiled=True)  54.4 us
    all_gather x1, waiting for transfers between devices, body(): full_rotation = lax.all_gather(rotation, 'band', axis=1, tiled=True)  43 us
    unnamed x17, local copies, waits for them, and re-layouts  28.1 us
    dot_general x1, matrix products, body(): jnp.einsum('rc,rb->cb', dense_proj, returned_rows, precision=lax.Precisio...  12.5 us
  transfers between devices with their start and end apart: 9, of which 4 were waited for; matrix products, arithmetic and copies ran while one was open for 21% of the time, Pallas kernels for 0%

commit v1 on v0

v1 whole, which is shorter than its diff:
```python
import functools

import jax
import jax.numpy as jnp
from jax import lax
from jax.experimental import pallas as pl
from jax.experimental.pallas import tpu as pltpu
from jax.sharding import PartitionSpec as P


F32, BF16 = jnp.float32, jnp.bfloat16
Y, Z, C = 4, 8, 2
OWN = 8
NP = 8
TILES = 128
TILE = 256
CELLS = 2048
PLANE = 1024
W = 256
STEP_TILES = 32
GROUP = 8
HI, LO = 8, 256
SLOTS = Y * Z * OWN
ALL = C * SLOTS
VMEM = 56 << 20


def split(x):
    hi = x.astype(BF16)
    return hi, (x - hi.astype(F32)).astype(BF16)


def dot3(a_hi, a_lo, b_hi, b_lo, dims):
    dot = functools.partial(
        lax.dot_general, dimension_numbers=(dims, ((), ())), preferred_element_type=F32
    )
    return dot(a_hi, b_hi) + (dot(a_lo, b_hi) + dot(a_hi, b_lo))


def slot_of(atom, owner_ref):
    me = lax.axis_index("dom")
    row = owner_ref[jnp.maximum(atom, 0)]
    owner = row // OWN
    core = jnp.bitwise_xor(owner, me) & 1
    y = (owner // (Z * C) - me // (Z * C)) & (Y - 1)
    z = (owner // C) & (Z - 1)
    slot = ((core * Y + y) * Z + z) * OWN + (row & (OWN - 1))
    return jnp.where(atom >= 0, slot, ALL)


def project_kernel(
    owner_ref, atom_ref, proj_ref, cell_ref, x_ref,
    keep_ref, send_ref, dhi_ref, dlo_ref, slot_ref,
    xhi_ref, xlo_ref, dense_ref, part_ref, sums_ref, mine_ref, sem,
):
    step = pl.program_id(0)

    @pl.when(step == 0)
    def _():
        first = pl.multiple_of(lax.axis_index("dom") * TILES, TILES)
        copy = pltpu.make_async_copy(atom_ref.at[pl.ds(first, TILES)], mine_ref, sem)
        copy.start()
        sums_ref[...] = jnp.zeros_like(sums_ref)
        hi, lo = split(x_ref[...])
        xhi_ref[...] = hi
        xlo_ref[...] = lo
        copy.wait()

    lo_ids = lax.broadcasted_iota(jnp.int32, (LO, TILE), 0).astype(F32).astype(BF16)
    pair_ids = (lax.broadcasted_iota(jnp.int32, (2 * NP, TILE), 0) // NP).astype(F32)
    one, zero = jnp.ones((), BF16), jnp.zeros((), BF16)

    def densify(group, carry):
        for i in range(GROUP):
            e = group * GROUP + i
            slot_ref[step * STEP_TILES + e] = slot_of(
                mine_ref[step * STEP_TILES + e], owner_ref
            )
            cells = cell_ref[pl.ds(e, 1), :]
            v_hi, v_lo = split(proj_ref[e])
            v_hi = jnp.concatenate([v_hi, v_hi], axis=0)
            v_lo = jnp.concatenate([v_lo, v_lo], axis=0)
            high = jnp.broadcast_to((cells // LO).astype(F32), (2 * NP, TILE)) - pair_ids
            high = high.astype(BF16)
            hits = [high == jnp.full((), 2.0 * h, BF16) for h in range(HI // 2)]
            spread = jnp.concatenate(
                [jnp.where(hit, v, zero) for v in (v_hi, v_lo) for hit in hits], axis=0
            )
            low = (cells & (LO - 1)).astype(F32).astype(BF16)
            hot = jnp.where(jnp.broadcast_to(low, (LO, TILE)) == lo_ids, one, zero)
            both = lax.dot_general(
                spread, hot, (((1,), (1,)), ((), ())), preferred_element_type=F32
            )
            sums = both[: HI * NP] + both[HI * NP :]
            rows = pl.ds(pl.multiple_of(e * NP, NP), NP)
            for h in range(HI):
                dense_ref[rows, h * LO : (h + 1) * LO] = sums[h * NP : (h + 1) * NP]
        return carry

    lax.fori_loop(0, STEP_TILES // GROUP, densify, 0)
    d_hi, d_lo = split(dense_ref[...])
    dhi_ref[...] = d_hi
    dlo_ref[...] = d_lo
    rows = STEP_TILES * NP
    dot = functools.partial(
        lax.dot_general, dimension_numbers=(((1,), (0,)), ((), ())), preferred_element_type=F32
    )
    upper = dot(jnp.concatenate([d_hi, d_lo], axis=0), xhi_ref[...])
    part_ref[...] = upper[:rows] + (upper[rows:] + dot(d_hi, xlo_ref[...]))

    def add(e, carry):
        slot = slot_ref[step * STEP_TILES + e]
        value = part_ref[pl.ds(pl.multiple_of(e * NP, NP), NP), :]
        sums_ref[slot] = sums_ref[slot] + value
        return carry

    lax.fori_loop(0, STEP_TILES, add, 0, unroll=8)

    @pl.when(step == TILES // STEP_TILES - 1)
    def _():
        keep_ref[...] = sums_ref[:SLOTS]
        send_ref[...] = sums_ref[SLOTS:ALL]


def project(tile_atom, atom_owner, projectors, tile_cells, x):
    rows = STEP_TILES * NP
    return pl.pallas_call(
        project_kernel,
        out_shape=(
            jax.ShapeDtypeStruct((SLOTS, NP, W), F32),
            jax.ShapeDtypeStruct((SLOTS, NP, W), F32),
            pltpu.HBM((TILES * NP, CELLS), BF16),
            pltpu.HBM((TILES * NP, CELLS), BF16),
            jax.ShapeDtypeStruct((TILES,), jnp.int32),
        ),
        grid_spec=pltpu.PrefetchScalarGridSpec(
            num_scalar_prefetch=1,
            grid=(TILES // STEP_TILES,),
            in_specs=[
                pl.BlockSpec(memory_space=pl.ANY),
                pl.BlockSpec((STEP_TILES, NP, TILE), lambda i, *_: (i, 0, 0)),
                pl.BlockSpec((STEP_TILES, TILE), lambda i, *_: (i, 0)),
                pl.BlockSpec((CELLS, W), lambda i, *_: (0, 0)),
            ],
            out_specs=[
                pl.BlockSpec((SLOTS, NP, W), lambda i, *_: (0, 0, 0)),
                pl.BlockSpec((SLOTS, NP, W), lambda i, *_: (0, 0, 0)),
                pl.BlockSpec((rows, CELLS), lambda i, *_: (i, 0)),
                pl.BlockSpec((rows, CELLS), lambda i, *_: (i, 0)),
                pl.BlockSpec(memory_space=pltpu.SMEM),
            ],
            scratch_shapes=[
                pltpu.VMEM((CELLS, W), BF16),
                pltpu.VMEM((CELLS, W), BF16),
                pltpu.VMEM((rows, CELLS), F32),
                pltpu.VMEM((rows, W), F32),
                pltpu.VMEM((ALL + 1, NP, W), F32),
                pltpu.SMEM((TILES,), jnp.int32),
                pltpu.SemaphoreType.DMA(()),
            ],
        ),
        compiler_params=pltpu.CompilerParams(vmem_limit_bytes=VMEM),
        name="project",
    )(atom_owner, tile_atom, projectors, tile_cells, x)


def couple_kernel(coupling_ref, sums_ref, out_ref):
    sums = sums_ref[0]
    for z in range(1, Z):
        sums = sums + sums_ref[z]
    for r in range(OWN):
        matrix = coupling_ref[r]
        total = matrix[:, 0:1] * sums[r, 0:1, :]
        for j in range(1, NP):
            total = total + matrix[:, j : j + 1] * sums[r, j : j + 1, :]
        out_ref[r * NP : (r + 1) * NP, :] = total


def couple(coupling, sums):
    return pl.pallas_call(
        couple_kernel, out_shape=jax.ShapeDtypeStruct((OWN * NP, W), F32), name="couple"
    )(coupling, sums)


def relative_rows(rotation_ref, offset):
    band = (lax.axis_index("band") + offset) & 3
    return rotation_ref[pl.ds(pl.multiple_of(band * W, W), W), :]


def turn_small_kernel(rotation_ref, mine_ref, right_ref, far_ref, left_ref, out_ref):
    total = None
    for offset, ref in enumerate((mine_ref, right_ref, far_ref, left_ref)):
        term = dot3(*split(ref[...]), *split(relative_rows(rotation_ref, offset)), ((1,), (0,)))
        total = term if total is None else total + term
    for z in range(Z):
        out_ref[z] = total


def turn_small(rotation, *pieces):
    return pl.pallas_call(
        turn_small_kernel, out_shape=jax.ShapeDtypeStruct((Z, OWN * NP, W), F32), name="turn_small"
    )(rotation, *pieces)


ROWS = 256


def turn_kernel(
    rotation_ref, mine_ref, right_a_ref, right_b_ref, left_a_ref, left_b_ref, far_a_ref,
    far_b_ref, out_ref, first_ref, second_ref, rhi_ref, rlo_ref, xhi_ref, xlo_ref,
):
    step = pl.program_id(0)
    low = step < PLANE // ROWS

    @pl.when(step == 0)
    def _():
        for offset in range(4):
            hi, lo = split(relative_rows(rotation_ref, offset))
            rhi_ref[offset * W : (offset + 1) * W, :] = hi
            rlo_ref[offset * W : (offset + 1) * W, :] = lo

    def of_plane(a_ref, b_ref):
        return jnp.where(low, a_ref[...], b_ref[...])

    values = (
        mine_ref[...],
        of_plane(right_a_ref, right_b_ref),
        of_plane(far_a_ref, far_b_ref),
        of_plane(left_a_ref, left_b_ref),
    )
    for offset, value in enumerate(values):
        hi, lo = split(value)
        xhi_ref[:, offset * W : (offset + 1) * W] = hi
        xlo_ref[:, offset * W : (offset + 1) * W] = lo
    result = dot3(xhi_ref[...], xlo_ref[...], rhi_ref[...], rlo_ref[...], ((1,), (0,)))
    out_ref[...] = result

    @pl.when(low)
    def _():
        first_ref[...] = result

    @pl.when(jnp.logical_not(low))
    def _():
        second_ref[...] = result


def turn(rotation, mine, right_a, right_b, left_a, left_b, far_a, far_b):
    half = PLANE // ROWS
    block = pl.BlockSpec((ROWS, W), lambda i: (i, 0))
    first = pl.BlockSpec((ROWS, W), lambda i: (jnp.minimum(i, half - 1), 0))
    second = pl.BlockSpec((ROWS, W), lambda i: (jnp.maximum(i - half, 0), 0))
    return pl.pallas_call(
        turn_kernel,
        out_shape=(
            jax.ShapeDtypeStruct((CELLS, W), F32),
            jax.ShapeDtypeStruct((PLANE, W), F32),
            jax.ShapeDtypeStruct((PLANE, W), F32),
        ),
        grid_spec=pl.GridSpec(
            grid=(CELLS // ROWS,),
            in_specs=[
                pl.BlockSpec((4 * W, W), lambda i: (0, 0)),
                block,
                first,
                second,
                first,
                second,
                first,
                second,
            ],
            out_specs=[block, first, second],
            scratch_shapes=[
                pltpu.VMEM((4 * W, W), BF16),
                pltpu.VMEM((4 * W, W), BF16),
                pltpu.VMEM((ROWS, 4 * W), BF16),
                pltpu.VMEM((ROWS, 4 * W), BF16),
            ],
        ),
        name="turn",
    )(rotation, mine, right_a, right_b, left_a, left_b, far_a, far_b)


def stencil_kernel(potential_ref, mine_ref, other_ref, out_ref):
    side = 32

    def line(y, carry):
        here = pl.ds(pl.multiple_of(y * side, side), side)
        above = pl.ds(pl.multiple_of(((y + side - 1) & (side - 1)) * side, side), side)
        below = pl.ds(pl.multiple_of(((y + 1) & (side - 1)) * side, side), side)
        value = mine_ref[here, :]
        beside = other_ref[here, :] + (mine_ref[above, :] + mine_ref[below, :])
        beside = beside + (pltpu.roll(value, 1, 0) + pltpu.roll(value, side - 1, 0))
        out_ref[here, :] = (3.0 + potential_ref[here, :]) * value - 0.5 * beside
        return carry

    lax.fori_loop(0, side, line, 0, unroll=4)


def stencil(potential, value):
    return pl.pallas_call(
        stencil_kernel,
        out_shape=jax.ShapeDtypeStruct((CELLS, W), F32),
        grid_spec=pl.GridSpec(
            grid=(2,),
            in_specs=[
                pl.BlockSpec((PLANE, 1), lambda i: (i, 0)),
                pl.BlockSpec((PLANE, W), lambda i: (i, 0)),
                pl.BlockSpec((PLANE, W), lambda i: (1 - i, 0)),
            ],
            out_specs=pl.BlockSpec((PLANE, W), lambda i: (i, 0)),
        ),
        name="stencil",
    )(potential, value, value)


PIECES = (64, 64, 32, 32, 64)


def expand_kernel(*refs):
    slot_ref, pieces = refs[0], refs[1:11]
    dhi_ref, dlo_ref, local_ref, before_ref, after_ref = refs[11:16]
    out_ref, all_ref, back_ref, bhi_ref, blo_ref, sems = refs[16:]
    step = pl.program_id(0)

    @pl.when(step == 0)
    def _():
        copies, start = [], 0
        for i, piece in enumerate(pieces):
            size = PIECES[i % len(PIECES)]
            copies.append(
                pltpu.make_async_copy(piece, all_ref.at[pl.ds(start, size)], sems.at[i])
            )
            start += size
        for copy in copies:
            copy.start()
        all_ref[ALL] = jnp.zeros((NP, W), F32)
        for copy in copies:
            copy.wait()

        def take(e, carry):
            back_ref[pl.ds(pl.multiple_of(e * NP, NP), NP), :] = all_ref[slot_ref[e]]
            return carry

        lax.fori_loop(0, TILES, take, 0, unroll=16)
        hi, lo = split(back_ref[...].T)
        bhi_ref[...] = hi
        blo_ref[...] = lo

    halo = jnp.where(step < PLANE // ROWS, before_ref[...], after_ref[...])
    far = dot3(bhi_ref[...], blo_ref[...], dhi_ref[...], dlo_ref[...], ((1,), (0,)))
    out_ref[...] = (local_ref[...] - 0.5 * halo) + far.T


def expand(slots, pieces, d_hi, d_lo, local, before, after):
    d_hi, d_lo, local = (
        pltpu.with_memory_space_constraint(v, pltpu.HBM) for v in (d_hi, d_lo, local)
    )
    half = PLANE // ROWS
    dense = pl.BlockSpec((TILES * NP, ROWS), lambda i, *_: (0, i))
    return pl.pallas_call(
        expand_kernel,
        out_shape=jax.ShapeDtypeStruct((CELLS, W), F32),
        grid_spec=pltpu.PrefetchScalarGridSpec(
            num_scalar_prefetch=1,
            grid=(CELLS // ROWS,),
            in_specs=[
                *[pl.BlockSpec(memory_space=pl.ANY)] * len(pieces),
                dense,
                dense,
                pl.BlockSpec((ROWS, W), lambda i, *_: (i, 0)),
                pl.BlockSpec((ROWS, W), lambda i, *_: (jnp.minimum(i, half - 1), 0)),
                pl.BlockSpec((ROWS, W), lambda i, *_: (jnp.maximum(i - half, 0), 0)),
            ],
            out_specs=pl.BlockSpec((ROWS, W), lambda i, *_: (i, 0)),
            scratch_shapes=[
                pltpu.VMEM((ALL + 1, NP, W), F32),
                pltpu.VMEM((TILES * NP, W), F32),
                pltpu.VMEM((W, TILES * NP), BF16),
                pltpu.VMEM((W, TILES * NP), BF16),
                pltpu.SemaphoreType.DMA((len(pieces),)),
            ],
        ),
        compiler_params=pltpu.CompilerParams(vmem_limit_bytes=20 << 20),
        name="expand",
    )(slots, *pieces, d_hi, d_lo, local, before, after)


def at(y, z, c):
    return (y % Y) * Z * C + (z % Z) * C + c


DEVICES = [(y, z, c) for y in range(Y) for z in range(Z) for c in range(C)]


def to_y(value, shift):
    return lax.ppermute(value, "dom", [(at(y, z, c), at(y + shift, z, c)) for y, z, c in DEVICES])


def to_core(value):
    return lax.ppermute(value, "dom", [(at(y, z, c), at(y, z, 1 - c)) for y, z, c in DEVICES])


def to_dom(value, shift):
    count = Y * Z * C
    return lax.ppermute(value, "dom", [(i, (i + shift) % count) for i in range(count)])


def to_band(value, shift):
    return lax.ppermute(value, "band", [(i, (i + shift) % 4) for i in range(4)])


Z_LINES = [[at(y, z, c) for z in range(Z)] for y in range(Y) for c in range(C)]


def swap_z(value):
    return lax.all_to_all(
        value, "dom", split_axis=0, concat_axis=0, axis_index_groups=Z_LINES, tiled=True
    )


def step(orbitals, potential, projectors, tile_cells, tile_atom, atom_owner, coupling, rotation):
    x = orbitals.reshape(CELLS, W)

    left_a = to_band(x[:PLANE], 1)
    right_b = to_band(x[PLANE:], -1)
    left_b = to_band(x[PLANE:], 1)
    right_a = to_band(x[:PLANE], -1)
    far_a = to_band(left_a, 1)
    far_b = to_band(right_b, -1)

    keep, send, d_hi, d_lo, slots = project(
        tile_atom, atom_owner, projectors, tile_cells, x
    )
    send = to_core(send)
    sums = (keep + send).reshape(Y, Z, OWN, NP, W)
    cut = Z // 2
    up = to_y(sums[2, :cut], 1)
    down = to_y(sums[2, cut:], -1)
    up_raw = to_y(sums[1, cut:], 1)
    down_raw = to_y(sums[3, :cut], -1)
    up = to_y(sums[1, :cut] + up, 1)
    down = to_y(sums[3, cut:] + down, -1)
    line = sums[0] + jnp.concatenate([up + down_raw, up_raw + down], axis=0)
    line = swap_z(line)
    scaled = couple(coupling, line)

    parts = to_band(scaled, -1), to_band(scaled, 2), to_band(scaled, 1)
    back = turn_small(rotation, scaled, *parts)

    line = swap_z(back).reshape(Z * OWN, NP, W)
    mid = Z * OWN // 2
    below_line = to_y(line, 1)
    above_line = to_y(line, -1)
    across_a = to_y(below_line[:mid], 1)
    across_b = to_y(above_line[mid:], -1)
    near = [line, above_line, across_a, across_b, below_line]
    pieces = near + [to_core(v) for v in near]

    turned, first, second = turn(
        rotation, x, right_a, right_b, left_a, left_b, far_a, far_b
    )
    before = to_dom(second, 1)
    after = to_dom(first, -1)
    local = stencil(potential.reshape(CELLS, 1), turned)
    applied = expand(slots, pieces, d_hi, d_lo, local, before, after)
    return turned.reshape(orbitals.shape), applied.reshape(orbitals.shape)


def solution(mesh):
    return jax.shard_map(
        step,
        mesh=mesh,
        in_specs=(
            P("dom", None, None, "band"),
            P("dom", None, None),
            P("dom", None, None),
            P("dom", None),
            P(),
            P(),
            P("dom", None, None),
            P(None, "band"),
        ),
        out_specs=(P("dom", None, None, "band"), P("dom", None, None, "band")),
        check_vma=False,
    )
```

time: 554 us -> 204 us (0.37)
  the two profiles are of different devices: /device:TPU:40 before, /device:TPU:1 now
where the time goes in v1:
time: 204 us; the launch traced here: 203 us
  waiting for transfers between devices  88.4 us (43%)
  starting transfers between devices  55.1 us (27%)
  Pallas kernels  50.6 us (25%)
  local copies, waits for them, and re-layouts  5.22 us (3%)
  other arithmetic  2.89 us (1%)
    ppermute x10, waiting for transfers between devices, to_y(): lax.ppermute(value, 'dom', [(at(y, z, c), at(y + shift, z, c)) for y, z,...  41.3 us
    ppermute x9, waiting for transfers between devices, to_band(): return lax.ppermute(value, 'band', [(i, (i + shift) % 4) for i in range(4)])  33.1 us
    pallas_call x1, Pallas kernels, project(): pl.pallas_call(project_kernel, out_shape=(jax.ShapeDtypeStruct((SLOTS, NP...  18.4 us
    ppermute x9, starting transfers between devices, to_band(): return lax.ppermute(value, 'band', [(i, (i + shift) % 4) for i in range(4)])  13.3 us
    all_to_all x2, starting transfers between devices, swap_z(): lax.all_to_all(value, 'dom', split_axis=0, concat_axis=0, axis_index_grou...  13 us
    pallas_call x1, Pallas kernels, expand(): pl.pallas_call(expand_kernel, out_shape=jax.ShapeDtypeStruct((CELLS, W),...  12.9 us
    ppermute x6, starting transfers between devices, to_core(): lax.ppermute(value, 'dom', [(at(y, z, c), at(y, z, 1 - c)) for y, z, c in...  11.5 us
    pallas_call x1, Pallas kernels, turn(): pl.pallas_call(turn_kernel, out_shape=(jax.ShapeDtypeStruct((CELLS, W), F...  10.5 us
  transfers between devices with their start and end apart: 29, of which 9 were waited for; matrix products, arithmetic and copies ran while one was open for 2% of the time, Pallas kernels for 9%

profile of v1, /device:TPU:1, one launch (start us, length us, event | category | flops | bytes accessed | tf_op | source)
XLA Modules:
  0.0 203.2 jit_solution(1842646342826074662)
XLA Ops:
  0.6 18.4 %project.1 = (f32[256,8,256]{2,1,0:T(8,128)}, f32[256,8,256]{2,1,0:T(8,128)}, bf16[1024,2048]{1,0:T(8,128)(2,1)}, bf16[1024,2048]{1,0:T(8,128)(2,1)}, s32[128]{0:T(128)}) custom-call(s32[512]{0:T(512)} %owner_ref.1, s32[8192]{0:T(1024)} %atom_ref.1, f32[128,8,256]{2,1,0:T(8,128)} %proj_ref.1, s32[128,256]{1,0:T(8,128)} %cell_ref.1, f32[2048,256]{1,0:T(8,128)} %bitcast.28), custom_call_target="tpu_custom_call" | custom-call | tf_op jit(solution)/shard_map/project/pallas_call | solution.py:127
  19.1 3.4 %collective-permute-start.6 = (f32[256,8,256]{2,1,0:T(8,128)}, f32[256,8,256]{2,1,0:T(8,128)S(1)}, u32[]{:S(2)}, u32[]{:S(2)}) collective-permute-start(f32[256,8,256]{2,1,0:T(8,128)} %get-tuple-element.13), channel_id=1, source_target_pairs={{0,1},{1,0},{2,3},{3,2},{4,5},{5,4},{6,7},{7,6},{8,9},{9,8},{10,11... | collective-permute-start | bytes 6291464 | tf_op jit(solution)/shard_map/ppermute | solution.py:400
  22.5 4.0 %collective-permute-done.6 = f32[256,8,256]{2,1,0:T(8,128)S(1)} collective-permute-done((f32[256,8,256]{2,1,0:T(8,128)}, f32[256,8,256]{2,1,0:T(8,128)S(1)}, u32[]{:S(2)}, u32[]{:S(2)}) %collective-permute-start.6) | collective-permute-done | bytes 2097184 | tf_op jit(solution)/shard_map/ppermute | solution.py:400
  26.5 1.9 add.18
  28.3 0.0 copy-start.1
  28.4 0.1 slice_bitcast_fusion.3
  28.4 0.1 collective-permute-start.10
  28.5 0.8 collective-permute-start.7
  29.4 1.9 collective-permute-start.11
  31.3 1.6 fusion.2
  32.8 2.0 collective-permute-start.1
  34.8 8.0 %collective-permute-done.7 = f32[4,8,8,256]{3,2,1,0:T(8,128)S(1)} collective-permute-done((f32[4,8,8,256]{3,2,1,0:T(8,128)S(1)}, f32[4,8,8,256]{3,2,1,0:T(8,128)S(1)}, u32[]{:S(2)}, u32[]{:S(2)}) %collective-permute-start.7) | collective-permute-done | bytes 262176 | tf_op jit(solution)/shard_map/ppermute | solution.py:396
  42.8 0.1 fusion.1
  42.9 0.3 collective-permute-start.12
  43.2 1.3 collective-permute-start.8
  44.6 10.5 %collective-permute-done.12 = f32[4,8,8,256]{3,2,1,0:T(8,128)S(1)} collective-permute-done((f32[4,8,8,256]{3,2,1,0:T(8,128)S(1)}, f32[4,8,8,256]{3,2,1,0:T(8,128)S(1)}, u32[]{:S(2)}, u32[]{:S(2)}) %collective-permute-start.12) | collective-permute-done | bytes 262176 | tf_op jit(solution)/shard_map/ppermute | solution.py:396
  55.2 0.9 maximum_add_fusion
  56.1 6.6 %all-to-all-start = ((f32[8,8,8,256]{3,2,1,0:T(8,128)}), f32[8,8,8,256]{3,2,1,0:T(8,128)S(1)}, u32[]{:S(2)}, u32[]{:S(2)}) async-start(f32[8,8,8,256]{3,2,1,0:T(8,128)} %maximum_add_fusion), calls=%async_computation | async-start | bytes 1048576 | tf_op jit(solution)/shard_map/all_to_all | solution.py:416
  62.7 2.5 %collective-permute-start = (f32[1024,256]{1,0:T(8,128)}, f32[1024,256]{1,0:T(8,128)}, u32[]{:S(2)}, u32[]{:S(2)}) collective-permute-start(f32[1024,256]{1,0:T(8,128)} %bitcast.1), channel_id=1, source_target_pairs={{0,192},{64,0},{128,64},{192,128},{1,193},{65,1},{129,65},{193,129... | collective-permute-start | bytes 3145736 | tf_op jit(solution)/shard_map/ppermute | solution.py:409
  65.2 0.3 collective-permute-start.4
  65.5 2.6 %collective-permute-start.5 = (f32[1024,256]{1,0:T(8,128)S(1)}, f32[1024,256]{1,0:T(8,128)}, u32[]{:S(2)}, u32[]{:S(2)}) collective-permute-start(f32[1024,256]{1,0:T(8,128)S(1)} %collective-permute-done.1.right_b_ref), channel_id=1, source_target_pairs={{0,192},{64,0},{128,64},{192,128},{1,193},{65,1},{129,65},{193,129... | collective-permute-start | bytes 3145736 | tf_op jit(solution)/shard_map/ppermute | solution.py:409
  68.2 10.0 %all-to-all-done.sums_ref = f32[8,8,8,256]{3,2,1,0:T(8,128)S(1)} async-done(((f32[8,8,8,256]{3,2,1,0:T(8,128)}), f32[8,8,8,256]{3,2,1,0:T(8,128)S(1)}, u32[]{:S(2)}, u32[]{:S(2)}) %all-to-all-start) | async-done | bytes 524320 | tf_op jit(solution)/shard_map/all_to_all | solution.py:416
  78.1 0.8 copy-done.2
  79.0 1.9 couple.1.mine_ref
  80.8 2.5 %collective-permute-start.13 = (f32[64,256]{1,0:T(8,128)}, f32[64,256]{1,0:T(8,128)S(1)}, u32[]{:S(2)}, u32[]{:S(2)}) collective-permute-start(f32[64,256]{1,0:T(8,128)} %couple.1.mine_ref), channel_id=1, source_target_pairs={{0,192},{64,0},{128,64},{192,128},{1,193},{65,1},{129,65},{193,129... | collective-permute-start | bytes 196616 | tf_op jit(solution)/shard_map/ppermute | solution.py:409
  83.4 26.3 %collective-permute-done.13.right_ref = f32[64,256]{1,0:T(8,128)S(1)} collective-permute-done((f32[64,256]{1,0:T(8,128)}, f32[64,256]{1,0:T(8,128)S(1)}, u32[]{:S(2)}, u32[]{:S(2)}) %collective-permute-start.13) | collective-permute-done | bytes 65568 | tf_op jit(solution)/shard_map/ppermute | solution.py:409
  109.7 2.4 %collective-permute-start.14 = (f32[64,256]{1,0:T(8,128)}, f32[64,256]{1,0:T(8,128)S(1)}, u32[]{:S(2)}, u32[]{:S(2)}) collective-permute-start(f32[64,256]{1,0:T(8,128)} %couple.1.mine_ref), channel_id=1, source_target_pairs={{0,128},{64,192},{128,0},{192,64},{1,129},{65,193},{129,1},{193,65... | collective-permute-start | bytes 196616 | tf_op jit(solution)/shard_map/ppermute | solution.py:409
  112.1 2.5 %collective-permute-done.14.far_ref = f32[64,256]{1,0:T(8,128)S(1)} collective-permute-done((f32[64,256]{1,0:T(8,128)}, f32[64,256]{1,0:T(8,128)S(1)}, u32[]{:S(2)}, u32[]{:S(2)}) %collective-permute-start.14) | collective-permute-done | bytes 65568 | tf_op jit(solution)/shard_map/ppermute | solution.py:409
  114.6 0.9 collective-permute-start.15
  115.5 4.3 %collective-permute-done.15.left_ref = f32[64,256]{1,0:T(8,128)S(1)} collective-permute-done((f32[64,256]{1,0:T(8,128)}, f32[64,256]{1,0:T(8,128)S(1)}, u32[]{:S(2)}, u32[]{:S(2)}) %collective-permute-start.15) | collective-permute-done | bytes 65568 | tf_op jit(solution)/shard_map/ppermute | solution.py:409
  119.8 0.6 copy-done.7
  120.4 2.6 %turn_small.1 = f32[8,64,256]{2,1,0:T(8,128)} custom-call(f32[1024,256]{1,0:T(8,128)} %rotation_ref.3, f32[64,256]{1,0:T(8,128)} %couple.1.mine_ref, f32[64,256]{1,0:T(8,128)} %copy-done.5, f32[64,256]{1,0:T(8,128)} %copy-done.6, f32[64,256]{1,0:T(8,128)} %copy-done.7), custom_call_target="tpu_custom_call" | custom-call | tf_op jit(solution)/shard_map/turn_small/pallas_call | solution.py:200
  123.0 6.4 %all-to-all-start.1 = ((f32[8,64,256]{2,1,0:T(8,128)}), f32[8,64,256]{2,1,0:T(8,128)S(1)}, u32[]{:S(2)}, u32[]{:S(2)}) async-start(f32[8,64,256]{2,1,0:T(8,128)} %turn_small.1), calls=%async_computation.1 | async-start | bytes 1048576 | tf_op jit(solution)/shard_map/all_to_all | solution.py:416
  129.4 10.5 %turn.1 = (f32[2048,256]{1,0:T(8,128)}, f32[1024,256]{1,0:T(8,128)}, f32[1024,256]{1,0:T(8,128)}) custom-call(f32[1024,256]{1,0:T(8,128)} %rotation_ref.3, f32[2048,256]{1,0:T(8,128)} %bitcast.29, f32[1024,256]{1,0:T(8,128)} %collective-permute-done.right_a_ref, f32[1024,256]{1,0:T(8,128)} %copy-done.3, f32[1024,256]{1,0:T(8,128)} %copy-done.4, ...), custom_call_target="tpu_custom_call" | custom-call | tf_op jit(solution)/shard_map/turn/pallas_call | solution.py:252
  139.8 7.2 %collective-permute-start.25 = (f32[1024,256]{1,0:T(8,128)}, f32[1024,256]{1,0:T(8,128)S(1)}, u32[]{:S(2)}, u32[]{:S(2)}) collective-permute-start(f32[1024,256]{1,0:T(8,128)} %get-tuple-element.16), channel_id=1, source_target_pairs={{0,1},{1,2},{2,3},{3,4},{4,5},{5,6},{6,7},{7,8},{8,9},{9,10},{10,1... | collective-permute-start | bytes 3145736 | tf_op jit(solution)/shard_map/ppermute | solution.py:405
  147.1 2.7 %collective-permute-start.16 = (f32[64,8,256]{2,1,0:T(8,128)S(1)}, f32[64,8,256]{2,1,0:T(8,128)S(1)}, u32[]{:S(2)}, u32[]{:S(2)}) collective-permute-start(f32[64,8,256]{2,1,0:T(8,128)S(1)} %bitcast.25), channel_id=1, source_target_pairs={{0,48},{1,49},{2,50},{3,51},{4,52},{5,53},{6,54},{7,55},{8,56},{9,... | collective-permute-start | bytes 1572872 | tf_op jit(solution)/shard_map/ppermute | solution.py:396
  149.8 4.0 %collective-permute-start.20 = (f32[64,8,256]{2,1,0:T(8,128)S(1)}, f32[64,8,256]{2,1,0:T(8,128)S(1)}, u32[]{:S(2)}, u32[]{:S(2)}) collective-permute-start(f32[64,8,256]{2,1,0:T(8,128)S(1)} %bitcast.26), channel_id=1, source_target_pairs={{0,1},{1,0},{2,3},{3,2},{4,5},{5,4},{6,7},{7,6},{8,9},{9,8},{10,11... | collective-permute-start | bytes 1572872 | tf_op jit(solution)/shard_map/ppermute | solution.py:400
  153.8 19.0 %collective-permute-done.17.refs_5_ = f32[64,8,256]{2,1,0:T(8,128)S(1)} collective-permute-done((f32[64,8,256]{2,1,0:T(8,128)S(1)}, f32[64,8,256]{2,1,0:T(8,128)S(1)}, u32[]{:S(2)}, u32[]{:S(2)}) %collective-permute-start.17) | collective-permute-done | bytes 524320 | tf_op jit(solution)/shard_map/ppermute | solution.py:396
  172.8 0.1 collective-permute-start.18
  172.9 1.2 collective-permute-start.21
  174.1 0.1 collective-permute-start.24
  174.2 2.9 %collective-permute-start.19 = (f32[32,8,256]{2,1,0:T(8,128)S(1)}, f32[32,8,256]{2,1,0:T(8,128)}, u32[]{:S(2)}, u32[]{:S(2)}) collective-permute-start(f32[32,8,256]{2,1,0:T(8,128)S(1)} %slice.63), channel_id=1, source_target_pairs={{0,48},{1,49},{2,50},{3,51},{4,52},{5,53},{6,54},{7,55},{8,56},{9,... | collective-permute-start | bytes 786440 | tf_op jit(solution)/shard_map/ppermute | solution.py:396
  177.2 3.7 %collective-permute-done.18.refs_3_ = f32[32,8,256]{2,1,0:T(8,128)S(1)} collective-permute-done((f32[32,8,256]{2,1,0:T(8,128)S(1)}, f32[32,8,256]{2,1,0:T(8,128)S(1)}, u32[]{:S(2)}, u32[]{:S(2)}) %collective-permute-start.18) | collective-permute-done | bytes 262176 | tf_op jit(solution)/shard_map/ppermute | solution.py:396
  180.9 1.9 collective-permute-start.22
  182.8 0.8 collective-permute-start.23
  183.7 2.0 %reshape.32.potential_ref = f32[2048,1]{1,0:T(8,128)} reshape(f32[2,32,32]{2,1,0:T(8,128)S(1)} %copy-done.8) | data formatting | bytes 16384 | tf_op jit(solution)/shard_map/reshape | solution.py:464
  185.7 4.3 %stencil.1.refs_13_ = f32[2048,256]{1,0:T(8,128)} custom-call(f32[2048,1]{1,0:T(8,128)} %reshape.32.potential_ref, f32[2048,256]{1,0:T(8,128)} %get-tuple-element.10.mine_ref.other_ref, f32[2048,256]{1,0:T(8,128)} %get-tuple-element.10.mine_ref.other_ref), custom_call_target="tpu_custom_call" | custom-call | tf_op jit(solution)/shard_map/stencil/pallas_call | solution.py:300
  190.1 12.9 %expand.1 = f32[2048,256]{1,0:T(8,128)} custom-call(s32[128]{0:T(128)S(1)} %copy-done, f32[64,8,256]{2,1,0:T(8,128)S(1)} %bitcast.27, f32[64,8,256]{2,1,0:T(8,128)S(1)} %collective-permute-done.16.refs_2_, f32[32,8,256]{2,1,0:T(8,128)S(1)} %collective-permute-done.18.refs_3_, f32[32,8,256]{2,1,0:T(8,128)} %collective-permute-done.19.refs_4_, ...), custom_call_target="tpu_custom_call" | custom-call | tf_op jit(solution)/shard_map/expand/pallas_call | solution.py:360
  (45 shorter events, 0.2 us)
Async XLA Ops:
  19.1 7.4 %collective-permute-start.6 = (f32[256,8,256]{2,1,0:T(8,128)}, f32[256,8,256]{2,1,0:T(8,128)S(1)}, u32[]{:S(2)}, u32[]{:S(2)}) collective-permute-start(f32[256,8,256]{2,1,0:T(8,128)} %get-tuple-element.13), channel_id=1, source_target_pairs={{0,1},{1,0},{2,3},{3,2},{4,5},{5,4},{6,7},{7,6},{8,9},{9,8},{10,11... | collective-permute-start | bytes 6291464 | tf_op jit(solution)/shard_map/ppermute | solution.py:400
  28.3 2.9 %copy-start.1 = (f32[2,32,32,256]{3,2,1,0:T(8,128)S(1)}, f32[2,32,32,256]{3,2,1,0:T(8,128)}, u32[]{:S(2)}) copy-start(f32[2,32,32,256]{3,2,1,0:T(8,128)} %param.8) | copy-start | bytes 6291460
  28.4 14.8 %collective-permute-start.10 = (f32[4,8,8,256]{3,2,1,0:T(8,128)S(1)}, f32[4,8,8,256]{3,2,1,0:T(8,128)S(1)}, u32[]{:S(2)}, u32[]{:S(2)}) collective-permute-start(f32[4,8,8,256]{3,2,1,0:T(8,128)S(1)} %get-tuple-element.20), channel_id=1, source_target_pairs={{0,16},{1,17},{2,18},{3,19},{4,20},{5,21},{6,22},{7,23},{8,24},{9,... | collective-permute-start | bytes 786440 | tf_op jit(solution)/shard_map/ppermute | solution.py:396
  28.5 14.3 %collective-permute-start.7 = (f32[4,8,8,256]{3,2,1,0:T(8,128)S(1)}, f32[4,8,8,256]{3,2,1,0:T(8,128)S(1)}, u32[]{:S(2)}, u32[]{:S(2)}) collective-permute-start(f32[4,8,8,256]{3,2,1,0:T(8,128)S(1)} %get-tuple-element.21), channel_id=1, source_target_pairs={{0,16},{1,17},{2,18},{3,19},{4,20},{5,21},{6,22},{7,23},{8,24},{9,... | collective-permute-start | bytes 786440 | tf_op jit(solution)/shard_map/ppermute | solution.py:396
  29.4 13.5 %collective-permute-start.11 = (f32[4,8,8,256]{3,2,1,0:T(8,128)S(1)}, f32[4,8,8,256]{3,2,1,0:T(8,128)S(1)}, u32[]{:S(2)}, u32[]{:S(2)}) collective-permute-start(f32[4,8,8,256]{3,2,1,0:T(8,128)S(1)} %get-tuple-element.19), channel_id=1, source_target_pairs={{0,48},{1,49},{2,50},{3,51},{4,52},{5,53},{6,54},{7,55},{8,56},{9,... | collective-permute-start | bytes 786440 | tf_op jit(solution)/shard_map/ppermute | solution.py:396
  32.8 32.7 %collective-permute-start.1 = (f32[1024,256]{1,0:T(8,128)}, f32[1024,256]{1,0:T(8,128)S(1)}, u32[]{:S(2)}, u32[]{:S(2)}) collective-permute-start(f32[1024,256]{1,0:T(8,128)} %bitcast.2), channel_id=1, source_target_pairs={{0,192},{64,0},{128,64},{192,128},{1,193},{65,1},{129,65},{193,129... | collective-permute-start | bytes 3145736 | tf_op jit(solution)/shard_map/ppermute | solution.py:409
  34.8 30.4 %collective-permute-start.2 = (f32[1024,256]{1,0:T(8,128)}, f32[1024,256]{1,0:T(8,128)S(1)}, u32[]{:S(2)}, u32[]{:S(2)}) collective-permute-start(f32[1024,256]{1,0:T(8,128)} %bitcast.1), channel_id=1, source_target_pairs={{0,64},{64,128},{128,192},{192,0},{1,65},{65,129},{129,193},{193,1... | collective-permute-start | bytes 3145736 | tf_op jit(solution)/shard_map/ppermute | solution.py:409
  42.8 12.3 %collective-permute-start.9 = (f32[4,8,8,256]{3,2,1,0:T(8,128)S(1)}, f32[4,8,8,256]{3,2,1,0:T(8,128)S(1)}, u32[]{:S(2)}, u32[]{:S(2)}) collective-permute-start(f32[4,8,8,256]{3,2,1,0:T(8,128)S(1)} %get-tuple-element.18), channel_id=1, source_target_pairs={{0,48},{1,49},{2,50},{3,51},{4,52},{5,53},{6,54},{7,55},{8,56},{9,... | collective-permute-start | bytes 786440 | tf_op jit(solution)/shard_map/ppermute | solution.py:396
  42.9 12.2 %collective-permute-start.12 = (f32[4,8,8,256]{3,2,1,0:T(8,128)S(1)}, f32[4,8,8,256]{3,2,1,0:T(8,128)S(1)}, u32[]{:S(2)}, u32[]{:S(2)}) collective-permute-start(f32[4,8,8,256]{3,2,1,0:T(8,128)S(1)} %get-tuple-element.23), channel_id=1, source_target_pairs={{0,48},{1,49},{2,50},{3,51},{4,52},{5,53},{6,54},{7,55},{8,56},{9,... | collective-permute-start | bytes 786440 | tf_op jit(solution)/shard_map/ppermute | solution.py:396
  43.2 11.9 %collective-permute-start.8 = (f32[4,8,8,256]{3,2,1,0:T(8,128)S(1)}, f32[4,8,8,256]{3,2,1,0:T(8,128)S(1)}, u32[]{:S(2)}, u32[]{:S(2)}) collective-permute-start(f32[4,8,8,256]{3,2,1,0:T(8,128)S(1)} %get-tuple-element.22), channel_id=1, source_target_pairs={{0,16},{1,17},{2,18},{3,19},{4,20},{5,21},{6,22},{7,23},{8,24},{9,... | collective-permute-start | bytes 786440 | tf_op jit(solution)/shard_map/ppermute | solution.py:396
  56.1 22.1 %all-to-all-start = ((f32[8,8,8,256]{3,2,1,0:T(8,128)}), f32[8,8,8,256]{3,2,1,0:T(8,128)S(1)}, u32[]{:S(2)}, u32[]{:S(2)}) async-start(f32[8,8,8,256]{3,2,1,0:T(8,128)} %maximum_add_fusion), calls=%async_computation | async-start | bytes 1048576 | tf_op jit(solution)/shard_map/all_to_all | solution.py:416
  62.7 66.6 %collective-permute-start = (f32[1024,256]{1,0:T(8,128)}, f32[1024,256]{1,0:T(8,128)}, u32[]{:S(2)}, u32[]{:S(2)}) collective-permute-start(f32[1024,256]{1,0:T(8,128)} %bitcast.1), channel_id=1, source_target_pairs={{0,192},{64,0},{128,64},{192,128},{1,193},{65,1},{129,65},{193,129... | collective-permute-start | bytes 3145736 | tf_op jit(solution)/shard_map/ppermute | solution.py:409
  65.2 64.1 %collective-permute-start.3 = (f32[1024,256]{1,0:T(8,128)}, f32[1024,256]{1,0:T(8,128)}, u32[]{:S(2)}, u32[]{:S(2)}) collective-permute-start(f32[1024,256]{1,0:T(8,128)} %bitcast.2), channel_id=1, source_target_pairs={{0,64},{64,128},{128,192},{192,0},{1,65},{65,129},{129,193},{193,1... | collective-permute-start | bytes 3145736 | tf_op jit(solution)/shard_map/ppermute | solution.py:409
  65.2 64.1 %copy-start.4 = (f32[1024,256]{1,0:T(8,128)}, f32[1024,256]{1,0:T(8,128)S(1)}, u32[]{:S(2)}) copy-start(f32[1024,256]{1,0:T(8,128)S(1)} %collective-permute-done.2.left_a_ref) | copy-start | bytes 3145732
  65.2 64.1 %collective-permute-start.4 = (f32[1024,256]{1,0:T(8,128)S(1)}, f32[1024,256]{1,0:T(8,128)}, u32[]{:S(2)}, u32[]{:S(2)}) collective-permute-start(f32[1024,256]{1,0:T(8,128)S(1)} %collective-permute-done.2.left_a_ref), channel_id=1, source_target_pairs={{0,64},{64,128},{128,192},{192,0},{1,65},{65,129},{129,193},{193,1... | collective-permute-start | bytes 3145736 | tf_op jit(solution)/shard_map/ppermute | solution.py:409
  65.5 63.9 %copy-start.3 = (f32[1024,256]{1,0:T(8,128)}, f32[1024,256]{1,0:T(8,128)S(1)}, u32[]{:S(2)}) copy-start(f32[1024,256]{1,0:T(8,128)S(1)} %collective-permute-done.1.right_b_ref) | copy-start | bytes 3145732
  65.5 63.8 %collective-permute-start.5 = (f32[1024,256]{1,0:T(8,128)S(1)}, f32[1024,256]{1,0:T(8,128)}, u32[]{:S(2)}, u32[]{:S(2)}) collective-permute-start(f32[1024,256]{1,0:T(8,128)S(1)} %collective-permute-done.1.right_b_ref), channel_id=1, source_target_pairs={{0,192},{64,0},{128,64},{192,128},{1,193},{65,1},{129,65},{193,129... | collective-permute-start | bytes 3145736 | tf_op jit(solution)/shard_map/ppermute | solution.py:409
  78.1 0.8 copy-start.2
  80.8 28.8 %collective-permute-start.13 = (f32[64,256]{1,0:T(8,128)}, f32[64,256]{1,0:T(8,128)S(1)}, u32[]{:S(2)}, u32[]{:S(2)}) collective-permute-start(f32[64,256]{1,0:T(8,128)} %couple.1.mine_ref), channel_id=1, source_target_pairs={{0,192},{64,0},{128,64},{192,128},{1,193},{65,1},{129,65},{193,129... | collective-permute-start | bytes 196616 | tf_op jit(solution)/shard_map/ppermute | solution.py:409
  109.7 10.1 %copy-start.5 = (f32[64,256]{1,0:T(8,128)}, f32[64,256]{1,0:T(8,128)S(1)}, u32[]{:S(2)}) copy-start(f32[64,256]{1,0:T(8,128)S(1)} %collective-permute-done.13.right_ref) | copy-start | bytes 196612
  109.7 4.9 %collective-permute-start.14 = (f32[64,256]{1,0:T(8,128)}, f32[64,256]{1,0:T(8,128)S(1)}, u32[]{:S(2)}, u32[]{:S(2)}) collective-permute-start(f32[64,256]{1,0:T(8,128)} %couple.1.mine_ref), channel_id=1, source_target_pairs={{0,128},{64,192},{128,0},{192,64},{1,129},{65,193},{129,1},{193,65... | collective-permute-start | bytes 196616 | tf_op jit(solution)/shard_map/ppermute | solution.py:409
  114.6 5.2 %copy-start.6 = (f32[64,256]{1,0:T(8,128)}, f32[64,256]{1,0:T(8,128)S(1)}, u32[]{:S(2)}) copy-start(f32[64,256]{1,0:T(8,128)S(1)} %collective-permute-done.14.far_ref) | copy-start | bytes 196612
  114.6 5.2 %collective-permute-start.15 = (f32[64,256]{1,0:T(8,128)}, f32[64,256]{1,0:T(8,128)S(1)}, u32[]{:S(2)}, u32[]{:S(2)}) collective-permute-start(f32[64,256]{1,0:T(8,128)} %couple.1.mine_ref), channel_id=1, source_target_pairs={{0,64},{64,128},{128,192},{192,0},{1,65},{65,129},{129,193},{193,1... | collective-permute-start | bytes 196616 | tf_op jit(solution)/shard_map/ppermute | solution.py:409
  119.8 0.6 copy-start.7
  123.0 24.1 %all-to-all-start.1 = ((f32[8,64,256]{2,1,0:T(8,128)}), f32[8,64,256]{2,1,0:T(8,128)S(1)}, u32[]{:S(2)}, u32[]{:S(2)}) async-start(f32[8,64,256]{2,1,0:T(8,128)} %turn_small.1), calls=%async_computation.1 | async-start | bytes 1048576 | tf_op jit(solution)/shard_map/all_to_all | solution.py:416
  129.3 54.4 %copy-start.8 = (f32[2,32,32]{2,1,0:T(8,128)S(1)}, f32[2,32,32]{2,1,0:T(8,128)}, u32[]{:S(2)}) copy-start(f32[2,32,32]{2,1,0:T(8,128)} %param.9) | copy-start | bytes 24580
  139.8 34.3 %collective-permute-start.25 = (f32[1024,256]{1,0:T(8,128)}, f32[1024,256]{1,0:T(8,128)S(1)}, u32[]{:S(2)}, u32[]{:S(2)}) collective-permute-start(f32[1024,256]{1,0:T(8,128)} %get-tuple-element.16), channel_id=1, source_target_pairs={{0,1},{1,2},{2,3},{3,4},{4,5},{5,6},{6,7},{7,8},{8,9},{9,10},{10,1... | collective-permute-start | bytes 3145736 | tf_op jit(solution)/shard_map/ppermute | solution.py:405
  147.1 27.1 %collective-permute-start.26 = (f32[1024,256]{1,0:T(8,128)}, f32[1024,256]{1,0:T(8,128)}, u32[]{:S(2)}, u32[]{:S(2)}) collective-permute-start(f32[1024,256]{1,0:T(8,128)} %get-tuple-element.17), channel_id=1, source_target_pairs={{0,63},{1,0},{2,1},{3,2},{4,3},{5,4},{6,5},{7,6},{8,7},{9,8},{10,9... | collective-permute-start | bytes 3145736 | tf_op jit(solution)/shard_map/ppermute | solution.py:405
  147.1 25.7 %collective-permute-start.17 = (f32[64,8,256]{2,1,0:T(8,128)S(1)}, f32[64,8,256]{2,1,0:T(8,128)S(1)}, u32[]{:S(2)}, u32[]{:S(2)}) collective-permute-start(f32[64,8,256]{2,1,0:T(8,128)S(1)} %bitcast.24), channel_id=1, source_target_pairs={{0,16},{1,17},{2,18},{3,19},{4,20},{5,21},{6,22},{7,23},{8,24},{9,... | collective-permute-start | bytes 1572872 | tf_op jit(solution)/shard_map/ppermute | solution.py:396
  147.1 25.8 %collective-permute-start.16 = (f32[64,8,256]{2,1,0:T(8,128)S(1)}, f32[64,8,256]{2,1,0:T(8,128)S(1)}, u32[]{:S(2)}, u32[]{:S(2)}) collective-permute-start(f32[64,8,256]{2,1,0:T(8,128)S(1)} %bitcast.25), channel_id=1, source_target_pairs={{0,48},{1,49},{2,50},{3,51},{4,52},{5,53},{6,54},{7,55},{8,56},{9,... | collective-permute-start | bytes 1572872 | tf_op jit(solution)/shard_map/ppermute | solution.py:396
  149.8 40.3 %collective-permute-start.20 = (f32[64,8,256]{2,1,0:T(8,128)S(1)}, f32[64,8,256]{2,1,0:T(8,128)S(1)}, u32[]{:S(2)}, u32[]{:S(2)}) collective-permute-start(f32[64,8,256]{2,1,0:T(8,128)S(1)} %bitcast.26), channel_id=1, source_target_pairs={{0,1},{1,0},{2,3},{3,2},{4,5},{5,4},{6,7},{7,6},{8,9},{9,8},{10,11... | collective-permute-start | bytes 1572872 | tf_op jit(solution)/shard_map/ppermute | solution.py:400
  172.8 8.1 %collective-permute-start.18 = (f32[32,8,256]{2,1,0:T(8,128)S(1)}, f32[32,8,256]{2,1,0:T(8,128)S(1)}, u32[]{:S(2)}, u32[]{:S(2)}) collective-permute-start(f32[32,8,256]{2,1,0:T(8,128)S(1)} %slice.62), channel_id=1, source_target_pairs={{0,16},{1,17},{2,18},{3,19},{4,20},{5,21},{6,22},{7,23},{8,24},{9,... | collective-permute-start | bytes 786440 | tf_op jit(solution)/shard_map/ppermute | solution.py:396
  172.9 17.1 %collective-permute-start.21 = (f32[64,8,256]{2,1,0:T(8,128)S(1)}, f32[64,8,256]{2,1,0:T(8,128)}, u32[]{:S(2)}, u32[]{:S(2)}) collective-permute-start(f32[64,8,256]{2,1,0:T(8,128)S(1)} %collective-permute-done.16.refs_2_), channel_id=1, source_target_pairs={{0,1},{1,0},{2,3},{3,2},{4,5},{5,4},{6,7},{7,6},{8,9},{9,8},{10,11... | collective-permute-start | bytes 1572872 | tf_op jit(solution)/shard_map/ppermute | solution.py:400
  174.1 16.0 %collective-permute-start.24 = (f32[64,8,256]{2,1,0:T(8,128)S(1)}, f32[64,8,256]{2,1,0:T(8,128)}, u32[]{:S(2)}, u32[]{:S(2)}) collective-permute-start(f32[64,8,256]{2,1,0:T(8,128)S(1)} %collective-permute-done.17.refs_5_), channel_id=1, source_target_pairs={{0,1},{1,0},{2,3},{3,2},{4,5},{5,4},{6,7},{7,6},{8,9},{9,8},{10,11... | collective-permute-start | bytes 1572872 | tf_op jit(solution)/shard_map/ppermute | solution.py:400
  174.2 8.6 %collective-permute-start.19 = (f32[32,8,256]{2,1,0:T(8,128)S(1)}, f32[32,8,256]{2,1,0:T(8,128)}, u32[]{:S(2)}, u32[]{:S(2)}) collective-permute-start(f32[32,8,256]{2,1,0:T(8,128)S(1)} %slice.63), channel_id=1, source_target_pairs={{0,48},{1,49},{2,50},{3,51},{4,52},{5,53},{6,54},{7,55},{8,56},{9,... | collective-permute-start | bytes 786440 | tf_op jit(solution)/shard_map/ppermute | solution.py:396
  180.9 9.2 %collective-permute-start.22 = (f32[32,8,256]{2,1,0:T(8,128)S(1)}, f32[32,8,256]{2,1,0:T(8,128)}, u32[]{:S(2)}, u32[]{:S(2)}) collective-permute-start(f32[32,8,256]{2,1,0:T(8,128)S(1)} %collective-permute-done.18.refs_3_), channel_id=1, source_target_pairs={{0,1},{1,0},{2,3},{3,2},{4,5},{5,4},{6,7},{7,6},{8,9},{9,8},{10,11... | collective-permute-start | bytes 786440 | tf_op jit(solution)/shard_map/ppermute | solution.py:400
  182.8 7.3 %collective-permute-start.23 = (f32[32,8,256]{2,1,0:T(8,128)}, f32[32,8,256]{2,1,0:T(8,128)}, u32[]{:S(2)}, u32[]{:S(2)}) collective-permute-start(f32[32,8,256]{2,1,0:T(8,128)} %collective-permute-done.19.refs_4_), channel_id=1, source_target_pairs={{0,1},{1,0},{2,3},{3,2},{4,5},{5,4},{6,7},{7,6},{8,9},{9,8},{10,11... | collective-permute-start | bytes 786440 | tf_op jit(solution)/shard_map/ppermute | solution.py:400
  185.7 4.4 %copy-start = (s32[128]{0:T(128)S(1)}, s32[128]{0:T(128)}, u32[]{:S(2)}) copy-start(s32[128]{0:T(128)} %get-tuple-element.11.refs_0_) | copy-start | bytes 1540
